TPU v7x, 256 devices: a whole 4x4x8 slice. The times are simulated.
256 devices in a mesh: fsdp: 16 (over x_hi, y, core), ep: 16 (over x_lo, z).
Axes of the slice: x: 4 (x_hi: 2, x_lo: 2; x = x_hi * 2 + x_lo), y: 4, z: 8, core: 2. Of those that a mesh axis runs over, the one named last changes fastest.
Arguments:
- tokens: bfloat16 [65536, 2048], P(('fsdp', 'ep')), may hold values from -6 to 6
- out_grad: bfloat16 [65536, 2048], P(('fsdp', 'ep')), may hold values from -4 to 4
- expert_ids: int32 [65536, 8], P(('fsdp', 'ep')), may hold values from 0 to 127, as said below
- gate_probs: bfloat16 [65536, 8], P(('fsdp', 'ep')), may hold values from 0.19921875 to 1
- w_gate: bfloat16 [2048, 16, 768], P('fsdp', 'ep'), may hold values from -0.125 to 0.125
- w_up: bfloat16 [2048, 16, 768], P('fsdp', 'ep'), may hold values from -0.125 to 0.125
- w_down: bfloat16 [2048, 16, 768], P('fsdp', 'ep'), may hold values from -0.21875 to 0.21875
Outputs:
- in_grad: bfloat16 [65536, 2048], P(('fsdp', 'ep'))
- gate_grad: bfloat16 [65536, 8], P(('fsdp', 'ep'))
- grad_gate: bfloat16 [2048, 16, 768], P('fsdp', 'ep')
- grad_up: bfloat16 [2048, 16, 768], P('fsdp', 'ep')
- grad_down: bfloat16 [2048, 16, 768], P('fsdp', 'ep')
Inputs may be any that keep to these rules, and one draw needn't show every extreme that they name: `expert_ids`: each token names 8 different experts. Among the 256 tokens of one device each expert below 16 is named by at most 32 tokens; in each group of devices that share an index of fsdp, one expert below 16 is named by exactly 32 tokens of every device of the group.
All inputs are finite; a program needn't handle non-finite values.
Results may differ from a plain program's by a relative error of at most 0.014.
Values may be sent and summed in bfloat16 or wider, within the bound.
A program may use at most 128 MiB of HBM per device.

v0:
```python
import jax
import jax.numpy as jnp
from jax import lax
from jax.sharding import PartitionSpec as P

MOST = 32


def expert_math(grad_rows, gate_rows, gate_pre, up_pre, back_proj):
    sigmoid_gate = jax.nn.sigmoid(gate_pre)
    silu_gate = gate_pre * sigmoid_gate
    activated = (silu_gate * up_pre).astype(jnp.bfloat16)
    pick_grad = jnp.sum(activated.astype(jnp.float32) * back_proj, axis=-1).astype(jnp.bfloat16)
    weight_col = gate_rows.astype(jnp.float32)[:, None]
    scaled_back = weight_col * back_proj
    gate_delta = (
        scaled_back * up_pre * sigmoid_gate * (1.0 + gate_pre * (1.0 - sigmoid_gate))
    ).astype(jnp.bfloat16)
    up_delta = (scaled_back * silu_gate).astype(jnp.bfloat16)
    scaled_grad = (weight_col * grad_rows.astype(jnp.float32)).astype(jnp.bfloat16)
    return (activated, pick_grad, gate_delta, up_delta, scaled_grad)


def leading_product(left, right):
    return lax.dot_general(
        left, right, (((0,), (0,)), ((), ())), preferred_element_type=jnp.float32
    )


def trailing_product(left, right):
    return lax.dot_general(
        left, right, (((1,), (1,)), ((), ())), preferred_element_type=jnp.float32
    )


def per_device(tokens, out_grad, expert_ids, gate_probs, w_gate, w_up, w_down):
    tok_count, model_width = tokens.shape
    hidden = w_gate.shape[2]
    experts_here = lax.axis_size("ep")
    capacity = MOST
    owners = lax.iota(jnp.int32, experts_here)
    matches = expert_ids[:, :, None] == owners[None, None, :]
    chosen = jnp.any(matches, axis=1)
    gate_pick = jnp.sum(jnp.where(matches, gate_probs[:, :, None].astype(jnp.float32), 0.0), axis=1)
    chosen_int = chosen.astype(jnp.int32)
    slot_rows = (jnp.cumsum(chosen_int, axis=0) - chosen_int).T
    placed = chosen.T[:, None, :] & (
        slot_rows[:, None, :] == lax.iota(jnp.int32, capacity)[None, :, None]
    )
    token_range = lax.iota(jnp.int32, tok_count)
    token_index = jnp.sum(jnp.where(placed, token_range[None, None, :], 0), axis=2)
    filled = jnp.any(placed, axis=2)
    send_tokens = jnp.where(filled[:, :, None], tokens[token_index], jnp.zeros((), jnp.bfloat16))
    send_grads = jnp.where(filled[:, :, None], out_grad[token_index], jnp.zeros((), jnp.bfloat16))
    send_gates = jnp.where(
        filled, jnp.take_along_axis(gate_pick.T, token_index, axis=1), 0.0
    ).astype(jnp.bfloat16)
    gathered = (
        lax.all_gather(w_gate, "fsdp", axis=0, tiled=True),
        lax.all_gather(w_up, "fsdp", axis=0, tiled=True),
        lax.all_gather(w_down, "fsdp", axis=0, tiled=True),
    )
    weight_in = jnp.concatenate([gathered[0][:, 0, :], gathered[1][:, 0, :]], axis=1)
    weight_out = gathered[2][:, 0, :]
    recv_tokens = lax.all_to_all(send_tokens, "ep", split_axis=0, concat_axis=0, tiled=True)
    recv_grads = lax.all_to_all(send_grads, "ep", split_axis=0, concat_axis=0, tiled=True)
    recv_gates = lax.all_to_all(send_gates, "ep", split_axis=0, concat_axis=0, tiled=True)
    slots = recv_tokens.shape[1]
    flat_tokens = recv_tokens.reshape(-1, model_width)
    flat_grads = recv_grads.reshape(-1, model_width)
    both_pre = jnp.dot(flat_tokens, weight_in, preferred_element_type=jnp.float32)
    back_proj = jnp.dot(flat_grads, weight_out, preferred_element_type=jnp.float32)
    activated, pick_grad, gate_delta, up_delta, scaled_grad = expert_math(
        flat_grads, recv_gates.reshape(-1), both_pre[:, :hidden], both_pre[:, hidden:], back_proj
    )
    deltas = jnp.concatenate([gate_delta, up_delta], axis=1)
    row_grads = trailing_product(deltas, weight_in).astype(jnp.bfloat16)
    back_rows, back_picks, recv_tokens, deltas, activated, scaled_grad = (
        lax.all_to_all(
            row_grads.reshape(experts_here, slots, model_width),
            "ep",
            split_axis=0,
            concat_axis=0,
            tiled=True,
        ),
        lax.all_to_all(
            pick_grad.reshape(experts_here, slots), "ep", split_axis=0, concat_axis=0, tiled=True
        ),
        recv_tokens,
        deltas.reshape(experts_here, slots, 2 * hidden),
        activated.reshape(experts_here, slots, hidden),
        scaled_grad.reshape(experts_here, slots, model_width),
    )
    flat_back = back_rows.reshape(-1, model_width).astype(jnp.float32)
    in_grad = jax.ops.segment_sum(
        jnp.where(filled.reshape(-1)[:, None], flat_back, 0.0),
        token_index.reshape(-1),
        num_segments=tok_count,
    ).astype(jnp.bfloat16)
    safe_slot = jnp.minimum(slot_rows, capacity - 1)
    pick_values = jnp.take_along_axis(back_picks, safe_slot, axis=1).astype(jnp.float32)
    gate_grad = jnp.sum(jnp.where(matches, pick_values.T[:, None, :], 0.0), axis=2).astype(
        jnp.bfloat16
    )
    rows_x = recv_tokens.reshape(-1, model_width)
    rows_delta = deltas.reshape(-1, 2 * hidden)
    rows_act = activated.reshape(-1, hidden)
    rows_scaled = scaled_grad.reshape(-1, model_width)
    term = jnp.concatenate(
        [leading_product(rows_x, rows_delta), leading_product(rows_scaled, rows_act)], axis=1
    )
    summed = lax.psum_scatter(
        term.astype(jnp.bfloat16), "fsdp", scatter_dimension=0, tiled=True
    ).astype(jnp.float32)
    grad_gate = summed[:, None, :hidden].astype(jnp.bfloat16)
    grad_up = summed[:, None, hidden : 2 * hidden].astype(jnp.bfloat16)
    grad_down = summed[:, None, 2 * hidden :].astype(jnp.bfloat16)
    return (in_grad, gate_grad, grad_gate, grad_up, grad_down)


def solution(mesh):
    in_specs = (
        P(("fsdp", "ep"), None),
        P(("fsdp", "ep"), None),
        P(("fsdp", "ep"), None),
        P(("fsdp", "ep"), None),
        P("fsdp", "ep", None),
        P("fsdp", "ep", None),
        P("fsdp", "ep", None),
    )
    out_specs = (
        P(("fsdp", "ep"), None),
        P(("fsdp", "ep"), None),
        P("fsdp", "ep", None),
        P("fsdp", "ep", None),
        P("fsdp", "ep", None),
    )
    return jax.shard_map(
        per_device, mesh=mesh, in_specs=in_specs, out_specs=out_specs, check_vma=False
    )
```

profile of v0, /device:TPU:33, one launch (start us, length us, event | category | flops | bytes accessed | tf_op | source)
XLA Modules:
  0.0 440.4 jit_solution(2187337769022640148)
XLA Ops:
  7.2 0.7 all-gather.6.cloned.1.call-update
  8.0 0.7 all-gather.8.cloned.1.call-update
  8.7 0.7 fusion.13
  9.4 0.6 reduce-window.6
  10.0 0.2 slice_reduce_fusion
  10.2 0.1 fusion.14
  10.3 0.4 select_reduce_fusion
  10.8 3.3 gather_fusion.1
  14.1 3.3 gather_fusion
  17.4 0.4 fusion.12
  17.8 4.7 %broadcast_select_fusion = (bf16[16,32,2048]{2,1,0:T(8,128)(2,1)}, bf16[16,32,2048]{2,1,0:T(8,128)(2,1)}) fusion(bf16[16,32,2048]{2,1,0:T(8,128)(2,1)} %bitcast.69, pred[16,32]{1,0:T(8,128)(4,1)S(1)} %fusion.12, bf16[16,32,2048]{2,1,0:T(8,128)(2,1)} %bitcast.70), kind=kLoop, calls=%fused_computation.20 | loop fusion | flops 2097152 | bytes 8389120 | tf_op jit(solution)/shard_map/jit(_where)/select_n | solution.py:53
  22.6 9.0 %all-to-all-start.2 = ((bf16[16,32,2048]{2,1,0:T(8,128)(2,1)}), bf16[16,32,2048]{2,1,0:T(8,128)(2,1)S(1)}, u32[]{:S(2)}, u32[]{:S(2)}) async-start(bf16[16,32,2048]{2,1,0:T(8,128)(2,1)} %get-tuple-element.43), calls=%async_computation.2 | async-start | bytes 4194304 | tf_op jit(solution)/shard_map/all_to_all | solution.py:65
  31.6 0.7 all-gather.4.cloned.1.call-update
  32.2 47.1 %all-to-all-done.2 = bf16[16,32,2048]{2,1,0:T(8,128)(2,1)S(1)} async-done(((bf16[16,32,2048]{2,1,0:T(8,128)(2,1)}), bf16[16,32,2048]{2,1,0:T(8,128)(2,1)S(1)}, u32[]{:S(2)}, u32[]{:S(2)}) %all-to-all-start.2) | async-done | bytes 2097184 | tf_op jit(solution)/shard_map/all_to_all | solution.py:65
  79.3 7.0 %all-to-all-start.1 = ((bf16[16,32,2048]{2,1,0:T(8,128)(2,1)}), bf16[16,32,2048]{2,1,0:T(8,128)(2,1)}, u32[]{:S(2)}, u32[]{:S(2)}) async-start(bf16[16,32,2048]{2,1,0:T(8,128)(2,1)} %get-tuple-element.44), calls=%async_computation.1 | async-start | bytes 4194304 | tf_op jit(solution)/shard_map/all_to_all | solution.py:66
  86.3 58.6 %all-gather.8.cloned.1.call-done = bf16[2048,1,768]{2,0,1:T(8,128)(2,1)} async-done(((bf16[128,1,768]{2,0,1:T(8,128)(2,1)}), bf16[2048,1,768]{2,0,1:T(8,128)(2,1)}) %all-gather.8.cloned.1.call-update) | async-done | bytes 3145744 | tf_op jit(solution)/shard_map/all_gather | solution.py:60
  144.9 8.0 %fusion.2 = f32[512,1536]{1,0:T(8,128)} fusion(bf16[512,2048]{1,0:T(8,128)(2,1)S(1)} %bitcast.72, bf16[2048,768]{1,0:T(8,128)(2,1)} %bitcast.82, bf16[2048,768]{1,0:T(8,128)(2,1)} %bitcast.80), kind=kOutput, calls=%fused_computation.12 | convolution fusion | flops 3233808384 | bytes 11534336 | tf_op jit(solution)/shard_map/dot_general | solution.py:71
  152.8 50.2 %all-gather.4.cloned.1.call-done = bf16[2048,1,768]{2,0,1:T(8,128)(2,1)} async-done(((bf16[128,1,768]{2,0,1:T(8,128)(2,1)}), bf16[2048,1,768]{2,0,1:T(8,128)(2,1)}) %all-gather.4.cloned.1.call-update) | async-done | bytes 3145744 | tf_op jit(solution)/shard_map/all_gather | solution.py:61
  203.1 6.7 %multiply_reduce_fusion = (bf16[512]{0:T(512)(128)(2,1)S(1)}, bf16[512,768]{1,0:T(8,128)(2,1)}, f32[512,768]{1,0:T(8,128)}) fusion(f32[512,1536]{1,0:T(8,128)} %fusion.2, bf16[512,2048]{1,0:T(8,128)(2,1)} %bitcast.6, bf16[2048,1,768]{2,0,1:T(8,128)(2,1)} %all-gather.4.cloned.1.call-done), kind=kOutput, calls=%fused_computation.23 | convolution fusion | flops 1614151168 | bytes 10748928 | tf_op jit(solution)/shard_map/dot_general | solution.py:72
  209.7 0.7 convert_element_type.114
  210.4 6.9 %all-to-all-start.4 = ((bf16[16,1,32]{2,1,0:T(2,128)(2,1)}), bf16[16,1,32]{2,1,0:T(2,128)(2,1)S(1)}, u32[]{:S(2)}, u32[]{:S(2)}) async-start(bf16[16,1,32]{2,1,0:T(2,128)(2,1)} %convert_element_type.114), calls=%async_computation.4 | async-start | bytes 16384 | tf_op jit(solution)/shard_map/all_to_all | solution.py:86
  217.5 6.0 %all-to-all-done.4 = bf16[16,1,32]{2,1,0:T(2,128)(2,1)S(1)} async-done(((bf16[16,1,32]{2,1,0:T(2,128)(2,1)}), bf16[16,1,32]{2,1,0:T(2,128)(2,1)S(1)}, u32[]{:S(2)}, u32[]{:S(2)}) %all-to-all-start.4) | async-done | bytes 1056 | tf_op jit(solution)/shard_map/all_to_all | solution.py:86
  223.5 34.6 %gather_fusion.3 = bf16[4096]{0:T(1024)(128)(2,1)S(1)} fusion(bf16[16,32]{1,0:T(8,128)(2,1)S(1)} %bitcast.66, s32[4096]{0:T(1024)S(1)} %bitcast.68), kind=kCustom, calls=%fused_computation.3 | custom fusion | bytes 49152 | tf_op jit(solution)/shard_map/jit(take_along_axis)/gather | solution.py:101
  258.2 0.6 select_reduce_fusion.1
  258.8 0.1 copy.48
  258.9 4.7 %gather_fusion.2 = bf16[512]{0:T(512)(128)(2,1)S(1)} fusion(bf16[16,256]{0,1:T(8,128)(2,1)S(1)} %bitcast.67, s32[512]{0:T(512)S(1)} %reshape.162), kind=kCustom, calls=%fused_computation.2 | custom fusion | bytes 6144 | tf_op jit(solution)/shard_map/jit(take_along_axis)/gather | solution.py:56
  263.7 9.9 %all_to_all.30 = bf16[16,1,32]{2,1,0:T(2,128)(2,1)S(1)} all-to-all(bf16[16,1,32]{2,1,0:T(2,128)(2,1)S(1)} %copy.49), channel_id=1, replica_groups=mesh['fsdp'=16,'ep'=16] {'ep'}, dimensions={0} | all-to-all | bytes 2048 | tf_op jit(solution)/shard_map/all_to_all | solution.py:67
  273.7 3.2 multiply_convert_fusion.4
  276.9 3.8 convolution_convert_fusion.1
  280.8 3.8 convolution_convert_fusion
  284.5 11.3 %pad_maximum_fusion = bf16[2048,2304]{0,1:T(8,128)(2,1)} fusion(bf16[2048,768]{0,1:T(8,128)(2,1)S(1)} %convolution_convert_fusion.1, bf16[2048,1536]{0,1:T(8,128)(2,1)S(1)} %convolution_convert_fusion), kind=kLoop, calls=%fused_computation.5 | loop fusion | flops 18874368 | bytes 18874368 | tf_op jit(solution)/shard_map/concatenate | solution.py:109
  295.9 12.6 %copy.54 = bf16[2048,2304]{1,0:T(8,128)(2,1)} copy(bf16[2048,2304]{0,1:T(8,128)(2,1)} %pad_maximum_fusion) | data formatting | bytes 18874368
  308.4 1.1 copy-done.5
  309.5 7.6 %fusion.5 = bf16[512,2048]{1,0:T(8,128)(2,1)} fusion(bf16[2048,768]{1,0:T(8,128)(2,1)} %bitcast.83, bf16[2048,768]{1,0:T(8,128)(2,1)} %bitcast.81, bf16[512,768]{1,0:T(8,128)(2,1)S(1)} %copy-done.5, bf16[512,768]{1,0:T(8,128)(2,1)S(1)} %get-tuple-element.36), kind=kOutput, calls=%fused_computation.16 | convolution fusion | flops 3238002688 | bytes 9961472 | tf_op jit(solution)/shard_map/dot_general | solution.py:31
  317.2 4.8 %all-to-all-start.3 = ((bf16[16,32,2048]{2,1,0:T(8,128)(2,1)}), bf16[16,32,2048]{2,1,0:T(8,128)(2,1)S(1)}, u32[]{:S(2)}, u32[]{:S(2)}) async-start(bf16[16,32,2048]{2,1,0:T(8,128)(2,1)} %bitcast.74), calls=%async_computation.3 | async-start | bytes 4194304 | tf_op jit(solution)/shard_map/all_to_all | solution.py:79
  321.9 0.1 broadcast_in_dim.98
  322.1 45.8 %all-to-all-done.3 = bf16[16,32,2048]{2,1,0:T(8,128)(2,1)S(1)} async-done(((bf16[16,32,2048]{2,1,0:T(8,128)(2,1)}), bf16[16,32,2048]{2,1,0:T(8,128)(2,1)S(1)}, u32[]{:S(2)}, u32[]{:S(2)}) %all-to-all-start.3) | async-done | bytes 2097184 | tf_op jit(solution)/shard_map/all_to_all | solution.py:79
  367.9 1.3 copy-done.3
  369.2 8.7 %scatter_custom_fusion = f32[256,2048]{1,0:T(8,128)S(1)} fusion(s32[512]{0:T(512)S(1)} %reshape.176, bf16[512,2048]{1,0:T(8,128)(2,1)} %bitcast.71, f32[]{:T(128)} %constant.15.clone.1, pred[512]{0:T(512)(128)(4,1)S(1)} %broadcast_in_dim.98), kind=kCustom, calls=%fused_computation.9 | custom fusion | flops 3145728 | bytes 4195840 | tf_op jit(solution)/shard_map/scatter-add | solution.py:95
  377.9 1.1 convert_element_type.101
  379.1 50.7 %reduce-scatter.4.cloned.1.call-done = bf16[128,2304]{1,0:T(8,128)(2,1)} async-done(((bf16[2048,2304]{1,0:T(8,128)(2,1)}), bf16[128,2304]{1,0:T(8,128)(2,1)}) %reduce-scatter.4.cloned.1.call-update) | async-done | bytes 589840
  429.7 1.2 fusion.18
  430.9 0.2 copy.59
  431.0 0.8 copy.53
  431.9 0.2 copy.58
  432.0 0.8 copy.52
  432.9 0.2 copy.57
  433.0 0.8 copy.51
  (41 shorter events, 0.8 us)
Async XLA Ops:
  7.2 3.6 copy-start
  7.2 79.1 %all-gather.6.cloned.1.call-start = ((), (), s32[]{:S(2)}) async-start(), calls=%async_computation.7 | async-start | bytes 3342336 | tf_op jit(solution)/shard_map/all_gather | solution.py:59
  7.9 136.9 %all-gather.8.cloned.1.call-start = ((), (), s32[]{:S(2)}) async-start(), calls=%async_computation.8 | async-start | bytes 3342336 | tf_op jit(solution)/shard_map/all_gather | solution.py:60
  10.8 3.4 copy-start.2
  22.6 56.7 %all-to-all-start.2 = ((bf16[16,32,2048]{2,1,0:T(8,128)(2,1)}), bf16[16,32,2048]{2,1,0:T(8,128)(2,1)S(1)}, u32[]{:S(2)}, u32[]{:S(2)}) async-start(bf16[16,32,2048]{2,1,0:T(8,128)(2,1)} %get-tuple-element.43), calls=%async_computation.2 | async-start | bytes 4194304 | tf_op jit(solution)/shard_map/all_to_all | solution.py:65
  31.5 171.5 %all-gather.4.cloned.1.call-start = ((), (), s32[]{:S(2)}) async-start(), calls=%async_computation.6 | async-start | bytes 3342336 | tf_op jit(solution)/shard_map/all_gather | solution.py:61
  79.3 73.5 %all-to-all-start.1 = ((bf16[16,32,2048]{2,1,0:T(8,128)(2,1)}), bf16[16,32,2048]{2,1,0:T(8,128)(2,1)}, u32[]{:S(2)}, u32[]{:S(2)}) async-start(bf16[16,32,2048]{2,1,0:T(8,128)(2,1)} %get-tuple-element.44), calls=%async_computation.1 | async-start | bytes 4194304 | tf_op jit(solution)/shard_map/all_to_all | solution.py:66
  203.1 14.4 %copy-start.7 = (bf16[256,8]{0,1:T(8,128)(2,1)S(1)}, bf16[256,8]{0,1:T(8,128)(2,1)}, u32[]{:S(2)}) copy-start(bf16[256,8]{0,1:T(8,128)(2,1)} %param.10) | copy-start | bytes 12292
  210.4 13.1 %all-to-all-start.4 = ((bf16[16,1,32]{2,1,0:T(2,128)(2,1)}), bf16[16,1,32]{2,1,0:T(2,128)(2,1)S(1)}, u32[]{:S(2)}, u32[]{:S(2)}) async-start(bf16[16,1,32]{2,1,0:T(2,128)(2,1)} %convert_element_type.114), calls=%async_computation.4 | async-start | bytes 16384 | tf_op jit(solution)/shard_map/all_to_all | solution.py:86
  217.4 212.4 %reduce-scatter.4.cloned.1.call-start = ((), (), s32[]{:S(2)}) async-start(), calls=%async_computation.9 | async-start | bytes 10027008
  223.5 34.6 %copy-start.6 = (s32[256,8]{0,1:T(8,128)S(1)}, s32[256,8]{0,1:T(8,128)}, u32[]{:S(2)}) copy-start(s32[256,8]{0,1:T(8,128)} %param.9) | copy-start | bytes 24580
  273.7 3.2 copy-start.8
  276.9 3.8 copy-start.4
  308.4 1.1 copy-start.5
  317.2 50.7 %all-to-all-start.3 = ((bf16[16,32,2048]{2,1,0:T(8,128)(2,1)}), bf16[16,32,2048]{2,1,0:T(8,128)(2,1)S(1)}, u32[]{:S(2)}, u32[]{:S(2)}) async-start(bf16[16,32,2048]{2,1,0:T(8,128)(2,1)} %bitcast.74), calls=%async_computation.3 | async-start | bytes 4194304 | tf_op jit(solution)/shard_map/all_to_all | solution.py:79
  367.9 1.3 copy-start.3
  377.9 55.9 %copy-start.1 = (bf16[256,2048]{1,0:T(8,128)(2,1)S(1)}, bf16[256,2048]{1,0:T(8,128)(2,1)}, u32[]{:S(2)}) copy-start(bf16[256,2048]{1,0:T(8,128)(2,1)} %param.7) | copy-start | bytes 3145732
Sparse Core Ops, SparseCore 0:
  10.8 69.5 all-gather.5
  83.2 61.6 all-gather.7
  147.6 55.3 all-gather.3
  308.6 121.1 reduce-scatter.3
where the time goes:
time: 442 us; the launch traced here: 440 us
  waiting for transfers between devices  260 us (59%)
  local copies, waits for them, and re-layouts  66.6 us (15%)
  other arithmetic  32 us (7%)
  matrix products  29.8 us (7%)
  starting transfers between devices  27.8 us (6%)
  between operations  14 us (3%)
  blocking collectives  9.86 us (2%)
    all_gather x1, waiting for transfers between devices, per_device(): lax.all_gather(w_up, 'fsdp', axis=0, tiled=True)  58.6 us
    unnamed x5, waiting for transfers between devices  52.7 us
    all_gather x1, waiting for transfers between devices, per_device(): lax.all_gather(w_down, 'fsdp', axis=0, tiled=True)  50.2 us
    all_to_all x1, waiting for transfers between devices, per_device(): lax.all_to_all(send_tokens, 'ep', split_axis=0, concat_axis=0, tiled=True)  47.1 us
    all_to_all x1, waiting for transfers between devices, per_device(): lax.all_to_all(row_grads.reshape(experts_here, slots, model_width), 'ep',...  45.8 us
    gather x2, local copies, waits for them, and re-layouts, per_device(): jnp.take_along_axis(back_picks, safe_slot, axis=1).astype(jnp.float32)  34.6 us
    unnamed x27, local copies, waits for them, and re-layouts  18 us
    concatenate x1, other arithmetic, per_device(): jnp.concatenate([leading_product(rows_x, rows_delta), leading_product(row...  11.3 us
  transfers between devices with their start and end apart: 8, of which 6 were waited for; matrix products, arithmetic and copies ran while one was open for 9% of the time, Pallas kernels for 0%

commit v1 on v0

v1 whole, which is shorter than its diff:
```python
import jax
import jax.numpy as jnp
from jax import lax
from jax.experimental import pallas as pl
from jax.experimental.pallas import tpu as pltpu
from jax.sharding import PartitionSpec as P

MESH = pl.DeviceIdType.MESH
BF = jnp.bfloat16
F32 = jnp.float32

MOST = 32
D = 2048
FF = 768
TOK = 256
N_EP = 16
N_Z = 8
ROWS = N_EP * MOST
SHARD = 128
CW = D + 128

OFFS = (
    (0, 0), (1, 0), (0, 1), (0, 7),
    (1, 1), (1, 7), (0, 2), (0, 6),
    (1, 2), (1, 6), (0, 3), (0, 5),
    (1, 3), (1, 5), (0, 4), (1, 4),
)
BLOCKS = ((0, 8), (8, 8))
CHIPS = ((1, 2), (1, 1), (1, 3), (1, 0), (0, 2), (0, 1), (0, 3), (0, 0))


def dot(a, b):
    return jnp.dot(a, b, preferred_element_type=F32)


def kernel(
    tok, og, ids_t, gp_t, ids, gp, wg, wu, wd,
    in_grad, gate_grad, gg, gu, gd,
    w, snd, rcv, xt, qt, dl, hh, cs, cr, tb, sb, ry, xs, rx, pm, ptm, gc,
    w_ss, w_rs, a_ss, a_rs, c_ss, c_rs, s_ss, s_rs, y_ss, y_rs, x_ss, x_rs,
):
    f = lax.axis_index("fsdp")
    e = lax.axis_index("ep")
    xh, y, c = f // 8, (f // 2) % 4, f % 2
    xl, z = e // N_Z, e % N_Z
    sends = []

    def fdev(dx, dy, dc):
        return ((((xh + dx) % 2) * 4 + (y + dy) % 4) * 2 + (c + dc) % 2, e)

    def owner(i, sign):
        dx, dz = OFFS[i]
        return ((xl + dx) % 2) * N_Z + (z + N_Z + sign * dz) % N_Z

    def copy(src, dst, ss, rs, dev):
        return pltpu.make_async_remote_copy(
            src_ref=src, dst_ref=dst, send_sem=ss, recv_sem=rs,
            device_id=dev, device_id_type=MESH,
        )

    def send(*args):
        cp = copy(*args)
        cp.start()
        sends.append(cp)

    def wrows(fs):
        return w.at[pl.ds(pl.multiple_of(fs * SHARD, SHARD), SHARD), :]

    barrier = pltpu.get_barrier_semaphore()
    peers = [(f, owner(i, 1)) for i in range(1, N_EP)]
    peers += [fdev(1, 0, 0), fdev(0, 1, 0), fdev(0, 2, 0), fdev(0, 3, 0), fdev(0, 0, 1)]
    for dev in peers:
        pl.semaphore_signal(barrier, inc=1, device_id=dev, device_id_type=MESH)

    own = pl.ds(pl.multiple_of(f * SHARD, SHARD), SHARD)
    w[own, 0:FF] = wg[...]
    w[own, FF:2 * FF] = wu[...]
    w[own, 2 * FF:] = wd[...]

    idt = ids_t[...]
    gpt = gp_t[...].astype(F32)
    chosen, gates = [], []
    for i in range(N_EP):
        match = idt == owner(i, 1)
        chosen.append(jnp.sum(jnp.where(match, 1.0, 0.0), axis=0, keepdims=True))
        gates.append(jnp.sum(jnp.where(match, gpt, 0.0), axis=0, keepdims=True))
    chosen_all = jnp.concatenate(chosen, axis=0)
    before = (
        lax.broadcasted_iota(jnp.int32, (TOK, TOK), 0)
        < lax.broadcasted_iota(jnp.int32, (TOK, TOK), 1)
    )
    place = dot(chosen_all.astype(BF), jnp.where(before, 1.0, 0.0).astype(BF))
    place = jnp.where(chosen_all > 0.5, place, -1.0)
    want = lax.broadcasted_iota(jnp.int32, (MOST, TOK), 0).astype(F32)
    for i in range(N_EP):
        hit = place[i:i + 1, :] == want
        pm[i * MOST:(i + 1) * MOST, :] = jnp.where(hit, 1.0, 0.0).astype(BF)
        gcol = jnp.sum(jnp.where(hit, gates[i], 0.0), axis=1, keepdims=True)
        gc[i * MOST:(i + 1) * MOST, :] = jnp.broadcast_to(gcol, (MOST, 128))

    pl.semaphore_wait(barrier, len(peers))

    send(wrows(f), wrows(f), w_ss.at[0], w_rs.at[0], fdev(1, 0, 0))
    for d in (1, 2, 3):
        send(wrows(f), wrows(f), w_ss.at[d], w_rs.at[d], fdev(0, d, 0))
    send(wrows(f), wrows(f), w_ss.at[7], w_rs.at[7], fdev(0, 0, 1))

    for half in (1, 0):
        rows = slice(half * 256, half * 256 + 256)
        pick = pm[rows, :]
        gcol = gc[rows, 0:1]
        for n in range(4):
            cols = slice(n * 512, n * 512 + 512)
            snd[rows, n * 512:n * 512 + 512] = dot(pick, tok[:, cols]).astype(BF)
            snd[rows, D + n * 512:D + n * 512 + 512] = (
                gcol * dot(pick, og[:, cols])
            ).astype(BF)
        for i in reversed(range(half * 8, half * 8 + 8)):
            part = pl.ds(i * MOST, MOST)
            if i == 0:
                rcv[part, :] = snd[part, :]
            else:
                send(
                    snd.at[part, :], rcv.at[part, :], a_ss.at[i - 1], a_rs.at[i - 1],
                    (f, owner(i, 1)),
                )
        ptm[:, rows] = pick.T

    def arrived(k, fs):
        copy(wrows(fs), wrows(fs), w_ss.at[0], w_rs.at[k], fdev(0, 0, 1)).wait_recv()

    far = fdev(1, 0, 0)[0]
    arrived(0, far)
    for d in (1, 2, 3):
        send(wrows(far), wrows(far), w_ss.at[3 + d], w_rs.at[3 + d], fdev(0, d, 0))
    send(wrows(far), wrows(far), w_ss.at[8], w_rs.at[8], fdev(0, 0, 1))
    for dx, base in ((0, 0), (1, 3)):
        for d in (1, 2, 3):
            fs = fdev(dx, 4 - d, 0)[0]
            arrived(base + d, fs)
            k = 8 + base + d
            send(wrows(fs), wrows(fs), w_ss.at[k], w_rs.at[k], fdev(0, 0, 1))
    arrived(7, fdev(0, 0, 1)[0])
    arrived(8, fdev(1, 0, 1)[0])
    for dx, base in ((0, 0), (1, 3)):
        for d in (1, 2, 3):
            arrived(8 + base + d, fdev(dx, 4 - d, 1)[0])

    for first, count in BLOCKS:
        for i in range(first, first + count):
            if i:
                part = pl.ds(i * MOST, MOST)
                copy(
                    snd.at[part, :], rcv.at[part, :], a_ss.at[i - 1], a_rs.at[i - 1],
                    (f, owner(i, 1)),
                ).wait_recv()
        n_rows = count * MOST
        rows = slice(first * MOST, first * MOST + n_rows)
        xt[:, rows] = rcv[rows, 0:D].T
        qt[:, rows] = rcv[rows, D:].T

        def hidden(n, pick_sum):
            at = pl.multiple_of(n * 256, 256)
            x = rcv[rows, 0:D]
            a = dot(x, w[:, pl.ds(at, 256)])
            b = dot(x, w[:, pl.ds(at + FF, 256)])
            r = dot(rcv[rows, D:], w[:, pl.ds(at + 2 * FF, 256)])
            s = jax.nn.sigmoid(a)
            silu = a * s
            h = (silu * b).astype(BF)
            hh[rows, pl.ds(at, 256)] = h
            dl[rows, pl.ds(at, 256)] = (r * b * s * (1.0 + a * (1.0 - s))).astype(BF)
            dl[rows, pl.ds(at + FF, 256)] = (r * silu).astype(BF)
            return pick_sum + jnp.sum(h.astype(F32) * r, axis=1, keepdims=True)

        pick_sum = lax.fori_loop(0, FF // 256, hidden, jnp.zeros((n_rows, 1), F32))
        cs[rows, D:] = jnp.broadcast_to(pick_sum, (n_rows, 128)).astype(BF)

        def back(m, carry):
            at = pl.multiple_of(m * 256, 256)
            cs[rows, pl.ds(at, 256)] = lax.dot_general(
                dl[rows, :], w[pl.ds(at, 256), 0:2 * FF], (((1,), (1,)), ((), ())),
                preferred_element_type=F32,
            ).astype(BF)
            return carry

        lax.fori_loop(0, D // 256, back, 0)
        for i in range(first, first + count):
            part = pl.ds(i * MOST, MOST)
            if i == 0:
                cr[part, :] = cs[part, :]
            else:
                send(
                    cs.at[part, :], cr.at[part, :], c_ss.at[i - 1], c_rs.at[i - 1],
                    (f, owner(i, -1)),
                )

    mine, other = pl.multiple_of(c * SHARD, SHARD), pl.multiple_of((1 - c) * SHARD, SHARD)

    def reduce_pair(j):
        dx, d = CHIPS[j]
        part = pl.ds(j * SHARD, SHARD)
        copy(
            tb.at[j, pl.ds(other, SHARD), :], sb.at[part, :], s_ss.at[j], s_rs.at[j],
            fdev(0, 0, 1),
        ).wait_recv()
        sb[part, :] = (
            sb[part, :].astype(F32) + tb[j, pl.ds(mine, SHARD), :].astype(F32)
        ).astype(BF)
        if d:
            k = dx * 3 + d - 1
            send(sb.at[part, :], ry.at[k], y_ss.at[k], y_rs.at[k], fdev(0, d, 0))

    for j, (dx, d) in enumerate(CHIPS):
        at = pl.multiple_of((((xh + dx) % 2) * 4 + (y + d) % 4) * 256, 256)
        tb[j, :, 0:2 * FF] = dot(xt[pl.ds(at, 256), :], dl[...]).astype(BF)
        tb[j, :, 2 * FF:] = dot(qt[pl.ds(at, 256), :], hh[...]).astype(BF)
        send(
            tb.at[j, pl.ds(other, SHARD), :], sb.at[pl.ds(j * SHARD, SHARD), :],
            s_ss.at[j], s_rs.at[j], fdev(0, 0, 1),
        )
        if j:
            reduce_pair(j - 1)
    reduce_pair(len(CHIPS) - 1)

    def y_sum(dx):
        j = CHIPS.index((dx, 0))
        total = sb[j * SHARD:(j + 1) * SHARD, :].astype(F32)
        for d in (1, 2, 3):
            k = dx * 3 + d - 1
            copy(ry.at[k], ry.at[k], y_ss.at[k], y_rs.at[k], fdev(0, d, 0)).wait_recv()
            total = total + ry[k].astype(F32)
        return total

    xs[...] = y_sum(1).astype(BF)
    send(xs, rx, x_ss, x_rs, fdev(1, 0, 0))

    lane = lax.broadcasted_iota(jnp.int32, (MOST, 128), 1)
    for i in range(N_EP):
        part = pl.ds(i * MOST, MOST)
        if i:
            copy(
                cs.at[part, :], cr.at[part, :], c_ss.at[i - 1], c_rs.at[i - 1],
                (f, owner(i, -1)),
            ).wait_recv()
        cr[part, D:] = jnp.where(lane == owner(i, 1), cr[part, D:], jnp.zeros((), BF))
    for n in range(4):
        cols = slice(n * 512, n * 512 + 512)
        in_grad[:, cols] = dot(ptm[...], cr[:, cols]).astype(BF)
    picks = dot(ptm[...], cr[:, D:])
    lanes = lax.broadcasted_iota(jnp.int32, (TOK, 128), 1)
    for k in range(8):
        got = jnp.where(ids[:, k:k + 1] == lanes, picks, 0.0)
        gate_grad[:, k:k + 1] = (
            jnp.sum(got, axis=1, keepdims=True) / gp[:, k:k + 1].astype(F32)
        ).astype(BF)

    total = y_sum(0)
    copy(xs, rx, x_ss, x_rs, fdev(1, 0, 0)).wait_recv()
    total = (total + rx[...].astype(F32)).astype(BF)
    gg[...] = total[:, 0:FF]
    gu[...] = total[:, FF:2 * FF]
    gd[...] = total[:, 2 * FF:]
    for cp in sends:
        cp.wait_send()


def per_device(tokens, out_grad, expert_ids, gate_probs, w_gate, w_up, w_down):
    vmem = pl.BlockSpec(memory_space=pltpu.VMEM)
    dma = pltpu.SemaphoreType.DMA
    outs = pl.pallas_call(
        kernel,
        out_shape=(
            jax.ShapeDtypeStruct((TOK, D), BF),
            jax.ShapeDtypeStruct((TOK, 8), BF),
        ) + (jax.ShapeDtypeStruct((SHARD, FF), BF),) * 3,
        in_specs=[vmem] * 9,
        out_specs=(vmem,) * 5,
        scratch_shapes=[
            pltpu.VMEM((D, 3 * FF), BF),
            pltpu.VMEM((ROWS, 2 * D), BF),
            pltpu.VMEM((ROWS, 2 * D), BF),
            pltpu.VMEM((D, ROWS), BF),
            pltpu.VMEM((D, ROWS), BF),
            pltpu.VMEM((ROWS, 2 * FF), BF),
            pltpu.VMEM((ROWS, FF), BF),
            pltpu.VMEM((ROWS, CW), BF),
            pltpu.VMEM((ROWS, CW), BF),
            pltpu.VMEM((8, 256, 3 * FF), BF),
            pltpu.VMEM((8 * SHARD, 3 * FF), BF),
            pltpu.VMEM((6, SHARD, 3 * FF), BF),
            pltpu.VMEM((SHARD, 3 * FF), BF),
            pltpu.VMEM((SHARD, 3 * FF), BF),
            pltpu.VMEM((ROWS, TOK), BF),
            pltpu.VMEM((TOK, ROWS), BF),
            pltpu.VMEM((ROWS, 128), F32),
            dma((15,)), dma((15,)), dma((15,)), dma((15,)), dma((15,)), dma((15,)),
            dma((8,)), dma((8,)), dma((6,)), dma((6,)), dma, dma,
        ],
        compiler_params=pltpu.CompilerParams(
            collective_id=0, has_side_effects=True, vmem_limit_bytes=62 * 2**20
        ),
        name="expert_backward",
    )(
        tokens, out_grad, expert_ids.T, gate_probs.T, expert_ids, gate_probs,
        w_gate[:, 0, :], w_up[:, 0, :], w_down[:, 0, :],
    )
    in_grad, gate_grad, g_gate, g_up, g_down = outs
    return in_grad, gate_grad, g_gate[:, None, :], g_up[:, None, :], g_down[:, None, :]


def solution(mesh):
    rows = P(("fsdp", "ep"), None)
    weight = P("fsdp", "ep", None)
    return jax.shard_map(
        per_device,
        mesh=mesh,
        in_specs=(rows,) * 4 + (weight,) * 3,
        out_specs=(rows,) * 2 + (weight,) * 3,
        check_vma=False,
    )
```

time: 442 us -> 192 us (0.43)
  waiting for transfers between devices: 260 us -> 0 us
  Pallas kernels: 0 us -> 181 us
  local copies, waits for them, and re-layouts: 66.6 us -> 8.73 us
  other arithmetic: 32 us -> 0 us
  matrix products: 29.8 us -> 0 us
  starting transfers between devices: 27.8 us -> 0 us
  between operations: 14 us -> 0.65 us
  blocking collectives: 9.86 us -> 0 us
    pallas_call x0 -> x1, Pallas kernels: none -> 181 us  [per_device(): pl.pallas_call(kernel, out_shape=(jax.ShapeDtypeStruct((TOK, D), BF), jax...]
    all_gather x3 -> x0, waiting for transfers between devices: 109 us -> none  [the longest x1 58.6 us: per_device(): lax.all_gather(w_up, 'fsdp', axis=0, tiled=True)]
    all_to_all x4 -> x0, waiting for transfers between devices: 98.9 us -> none  [the longest x1 47.1 us: per_device(): lax.all_to_all(send_tokens, 'ep', split_axis=0, concat_axis=0, tiled=True)]
    unnamed x5 -> x0, waiting for transfers between devices: 52.7 us -> none
    gather x7 -> x0, local copies, waits for them, and re-layouts: 46.1 us -> none  [the longest x2 34.6 us: per_device(): jnp.take_along_axis(back_picks, safe_slot, axis=1).astype(jnp.float32)]
    dot_general x5 -> x0, matrix products: 29.8 us -> none  [the longest x1 7.95 us: per_device(): jnp.dot(flat_tokens, weight_in, preferred_element_type=jnp.float32)]
    all_to_all x4 -> x0, starting transfers between devices: 27.6 us -> none  [the longest x1 8.95 us: per_device(): lax.all_to_all(send_tokens, 'ep', split_axis=0, concat_axis=0, tiled=True)]
    concatenate x1 -> x0, other arithmetic: 11.3 us -> none  [per_device(): jnp.concatenate([leading_product(rows_x, rows_delta), leading_product(row...]
  transfers between devices with their start and end apart: 8 -> 0, of which waited for: 6 -> 0; matrix products, arithmetic and copies ran while one was open for 9% -> 0% of each run, Pallas kernels for 0% -> 0%
where the time goes in v1:
time: 192 us; the launch traced here: 190 us
  Pallas kernels  181 us (94%)
  local copies, waits for them, and re-layouts  8.73 us (5%)
    pallas_call x1, Pallas kernels, per_device(): pl.pallas_call(kernel, out_shape=(jax.ShapeDtypeStruct((TOK, D), BF), jax...  181 us
    unnamed x17, local copies, waits for them, and re-layouts  8.73 us

profile of v1, /device:TPU:33, one launch (start us, length us, event | category | flops | bytes accessed | tf_op | source)
XLA Modules:
  0.0 190.5 jit_solution(14319132151454835234)
XLA Ops:
  0.6 0.0 copy-start.4
  0.6 0.7 copy-done.4
  1.3 0.0 copy-start.3
  1.3 0.7 copy.13.gp
  2.1 0.0 copy-done.3
  2.1 0.8 copy.12.ids
  2.8 181.1 %expert_backward.1 = (bf16[256,2048]{1,0:T(8,128)(2,1)}, bf16[256,8]{1,0:T(8,128)(2,1)}, bf16[128,768]{1,0:T(8,128)(2,1)}, bf16[128,768]{1,0:T(8,128)(2,1)}, bf16[128,768]{1,0:T(8,128)(2,1)}) custom-call(bf16[256,2048]{1,0:T(8,128)(2,1)} %tok.1, bf16[256,2048]{1,0:T(8,128)(2,1)} %og.1, s32[8,256]{1,0:T(8,128)} %bitcast.14, bf16[8,256]{1,0:T(8,128)(2,1)} %bitcast.15, ...), custom_call_target="tpu_custom_call" | custom-call | tf_op jit(solution)/shard_map/expert_backward/pallas_call | solution.py:271
  184.0 1.5 copy.14
  185.5 0.0 copy-start.2
  185.5 2.3 %copy.19 = bf16[256,2048]{1,0:T(8,128)(2,1)} copy(bf16[256,2048]{1,0:T(8,128)(2,1)} %get-tuple-element.25) | data formatting | bytes 2097152
  187.8 0.0 copy-done.2
  187.8 0.0 copy-start.1
  187.8 0.7 copy.20
  188.5 0.3 copy-done.1
  188.8 0.0 copy-start
  188.8 0.7 copy.21
  189.5 0.3 copy-done
  189.8 0.7 copy.22
Async XLA Ops:
  0.6 0.7 copy-start.4
  1.3 0.7 copy-start.3
  185.5 2.3 %copy-start.2 = (bf16[128,768]{1,0:T(8,128)(2,1)S(1)}, bf16[128,768]{1,0:T(8,128)(2,1)}, u32[]{:S(2)}) copy-start(bf16[128,768]{1,0:T(8,128)(2,1)} %get-tuple-element.12) | copy-start | bytes 589828
  187.8 1.0 copy-start.1
  188.8 1.0 copy-start

commit v2 on v1

--- a/solution.py
+++ b/solution.py
@@ -17,6 +17,7 @@
 N_Z = 8
 ROWS = N_EP * MOST
 SHARD = 128
+HALF = SHARD // 2
 CW = D + 128
 
 OFFS = (
@@ -25,8 +26,8 @@
     (1, 2), (1, 6), (0, 3), (0, 5),
     (1, 3), (1, 5), (0, 4), (1, 4),
 )
-BLOCKS = ((0, 8), (8, 8))
-CHIPS = ((1, 2), (1, 1), (1, 3), (1, 0), (0, 2), (0, 1), (0, 3), (0, 0))
+BLOCKS = ((0, 8), (8, 4), (12, 4))
+CHIPS = ((1, 2), (0, 2), (1, 1), (1, 3), (0, 1), (0, 3), (1, 0), (0, 0))
 
 
 def dot(a, b):
@@ -34,10 +35,10 @@
 
 
 def kernel(
-    tok, og, ids_t, gp_t, ids, gp, wg, wu, wd,
+    tok, og, ids_t, gp_t, wg, wu, wd,
     in_grad, gate_grad, gg, gu, gd,
-    w, snd, rcv, xt, qt, dl, hh, cs, cr, tb, sb, ry, xs, rx, pm, ptm, gc,
-    w_ss, w_rs, a_ss, a_rs, c_ss, c_rs, s_ss, s_rs, y_ss, y_rs, x_ss, x_rs,
+    w, snd, rcv, xt, qt, dl, hh, cs, cr, tb, sb, rf, ry, xs, rx, pm, ptm, gc,
+    w_ss, w_rs, a_ss, a_rs, c_ss, c_rs, s_ss, s_rs, f_ss, f_rs, y_ss, y_rs, x_ss, x_rs,
 ):
     f = lax.axis_index("fsdp")
     e = lax.axis_index("ep")
@@ -105,7 +106,7 @@
         send(wrows(f), wrows(f), w_ss.at[d], w_rs.at[d], fdev(0, d, 0))
     send(wrows(f), wrows(f), w_ss.at[7], w_rs.at[7], fdev(0, 0, 1))
 
-    for half in (1, 0):
+    for half in (0, 1):
         rows = slice(half * 256, half * 256 + 256)
         pick = pm[rows, :]
         gcol = gc[rows, 0:1]
@@ -115,7 +116,7 @@
             snd[rows, D + n * 512:D + n * 512 + 512] = (
                 gcol * dot(pick, og[:, cols])
             ).astype(BF)
-        for i in reversed(range(half * 8, half * 8 + 8)):
+        for i in range(half * 8, half * 8 + 8):
             part = pl.ds(i * MOST, MOST)
             if i == 0:
                 rcv[part, :] = snd[part, :]
@@ -204,11 +205,23 @@
             tb.at[j, pl.ds(other, SHARD), :], sb.at[part, :], s_ss.at[j], s_rs.at[j],
             fdev(0, 0, 1),
         ).wait_recv()
-        sb[part, :] = (
-            sb[part, :].astype(F32) + tb[j, pl.ds(mine, SHARD), :].astype(F32)
-        ).astype(BF)
-        if d:
-            k = dx * 3 + d - 1
+        for way, step in ((0, 1), (1, 3)):
+            half = pl.ds(j * SHARD + way * HALF, HALF)
+            total = (
+                sb[half, :].astype(F32)
+                + tb[j, pl.ds(mine + way * HALF, HALF), :].astype(F32)
+            )
+            k = dx * 2 + way
+            if d == step:
+                copy(
+                    rf.at[k], rf.at[k], f_ss.at[k], f_rs.at[k], fdev(0, d, 0)
+                ).wait_recv()
+                total = total + rf[k].astype(F32)
+            sb[half, :] = total.astype(BF)
+            if d == 2:
+                send(sb.at[half, :], rf.at[k], f_ss.at[k], f_rs.at[k], fdev(0, step, 0))
+        if d in (1, 3):
+            k = dx * 2 + d // 2
             send(sb.at[part, :], ry.at[k], y_ss.at[k], y_rs.at[k], fdev(0, d, 0))
 
     for j, (dx, d) in enumerate(CHIPS):
@@ -219,16 +232,16 @@
             tb.at[j, pl.ds(other, SHARD), :], sb.at[pl.ds(j * SHARD, SHARD), :],
             s_ss.at[j], s_rs.at[j], fdev(0, 0, 1),
         )
-        if j:
+        if j in (1, 2):
             reduce_pair(j - 1)
-    reduce_pair(len(CHIPS) - 1)
+    for j in range(2, len(CHIPS)):
+        reduce_pair(j)
 
     def y_sum(dx):
         j = CHIPS.index((dx, 0))
         total = sb[j * SHARD:(j + 1) * SHARD, :].astype(F32)
-        for d in (1, 2, 3):
-            k = dx * 3 + d - 1
-            copy(ry.at[k], ry.at[k], y_ss.at[k], y_rs.at[k], fdev(0, d, 0)).wait_recv()
+        for k in (2 * dx, 2 * dx + 1):
+            copy(ry.at[k], ry.at[k], y_ss.at[k], y_rs.at[k], fdev(0, 1, 0)).wait_recv()
             total = total + ry[k].astype(F32)
         return total
 
@@ -247,13 +260,11 @@
     for n in range(4):
         cols = slice(n * 512, n * 512 + 512)
         in_grad[:, cols] = dot(ptm[...], cr[:, cols]).astype(BF)
-    picks = dot(ptm[...], cr[:, D:])
-    lanes = lax.broadcasted_iota(jnp.int32, (TOK, 128), 1)
-    for k in range(8):
-        got = jnp.where(ids[:, k:k + 1] == lanes, picks, 0.0)
-        gate_grad[:, k:k + 1] = (
-            jnp.sum(got, axis=1, keepdims=True) / gp[:, k:k + 1].astype(F32)
-        ).astype(BF)
+    picks = dot(ptm[...], cr[:, D:]).T
+    got = jnp.zeros((8, TOK), F32)
+    for expert in range(N_EP):
+        got = got + jnp.where(idt == expert, picks[expert:expert + 1, :], 0.0)
+    gate_grad[...] = (got / gpt).astype(BF)
 
     total = y_sum(0)
     copy(xs, rx, x_ss, x_rs, fdev(1, 0, 0)).wait_recv()
@@ -272,9 +283,9 @@
         kernel,
         out_shape=(
             jax.ShapeDtypeStruct((TOK, D), BF),
-            jax.ShapeDtypeStruct((TOK, 8), BF),
+            jax.ShapeDtypeStruct((8, TOK), BF),
         ) + (jax.ShapeDtypeStruct((SHARD, FF), BF),) * 3,
-        in_specs=[vmem] * 9,
+        in_specs=[vmem] * 7,
         out_specs=(vmem,) * 5,
         scratch_shapes=[
             pltpu.VMEM((D, 3 * FF), BF),
@@ -288,25 +299,26 @@
             pltpu.VMEM((ROWS, CW), BF),
             pltpu.VMEM((8, 256, 3 * FF), BF),
             pltpu.VMEM((8 * SHARD, 3 * FF), BF),
-            pltpu.VMEM((6, SHARD, 3 * FF), BF),
+            pltpu.VMEM((4, HALF, 3 * FF), BF),
+            pltpu.VMEM((4, SHARD, 3 * FF), BF),
             pltpu.VMEM((SHARD, 3 * FF), BF),
             pltpu.VMEM((SHARD, 3 * FF), BF),
             pltpu.VMEM((ROWS, TOK), BF),
             pltpu.VMEM((TOK, ROWS), BF),
             pltpu.VMEM((ROWS, 128), F32),
             dma((15,)), dma((15,)), dma((15,)), dma((15,)), dma((15,)), dma((15,)),
-            dma((8,)), dma((8,)), dma((6,)), dma((6,)), dma, dma,
+            dma((8,)), dma((8,)), dma((4,)), dma((4,)), dma((4,)), dma((4,)), dma, dma,
         ],
         compiler_params=pltpu.CompilerParams(
             collective_id=0, has_side_effects=True, vmem_limit_bytes=62 * 2**20
         ),
         name="expert_backward",
     )(
-        tokens, out_grad, expert_ids.T, gate_probs.T, expert_ids, gate_probs,
+        tokens, out_grad, expert_ids.T, gate_probs.T,
         w_gate[:, 0, :], w_up[:, 0, :], w_down[:, 0, :],
     )
     in_grad, gate_grad, g_gate, g_up, g_down = outs
-    return in_grad, gate_grad, g_gate[:, None, :], g_up[:, None, :], g_down[:, None, :]
+    return in_grad, gate_grad.T, g_gate[:, None, :], g_up[:, None, :], g_down[:, None, :]
 
 
 def solution(mesh):

time: 192 us -> 172 us (0.90)
  Pallas kernels: 181 us -> 165 us
  local copies, waits for them, and re-layouts: 8.73 us -> 5.61 us
    pallas_call x1, Pallas kernels: 181 us -> 165 us  [per_device(): pl.pallas_call(kernel, out_shape=(jax.ShapeDtypeStruct((TOK, D), BF), jax...]
    unnamed x17 -> x13, local copies, waits for them, and re-layouts: 8.73 us -> 5.61 us
where the time goes in v2:
time: 172 us; the launch traced here: 171 us
  Pallas kernels  165 us (96%)
  local copies, waits for them, and re-layouts  5.61 us (3%)
    pallas_call x1, Pallas kernels, per_device(): pl.pallas_call(kernel, out_shape=(jax.ShapeDtypeStruct((TOK, D), BF), jax...  165 us
    unnamed x13, local copies, waits for them, and re-layouts  5.61 us

profile of v2, /device:TPU:33, one launch (start us, length us, event | category | flops | bytes accessed | tf_op | source)
XLA Modules:
  0.0 171.4 jit_solution(16473646360667403112)
XLA Ops:
  0.6 165.2 %expert_backward.1 = (bf16[256,2048]{1,0:T(8,128)(2,1)}, bf16[8,256]{1,0:T(8,128)(2,1)}, bf16[128,768]{1,0:T(8,128)(2,1)}, bf16[128,768]{1,0:T(8,128)(2,1)}, bf16[128,768]{1,0:T(8,128)(2,1)}) custom-call(bf16[256,2048]{1,0:T(8,128)(2,1)} %tok.1, bf16[256,2048]{1,0:T(8,128)(2,1)} %og.1, s32[8,256]{1,0:T(8,128)} %bitcast.15, bf16[8,256]{1,0:T(8,128)(2,1)} %bitcast.16, ...), custom_call_target="tpu_custom_call" | custom-call | tf_op jit(solution)/shard_map/expert_backward/pallas_call | solution.py:282
  165.8 0.0 copy-start.3
  165.8 0.0 copy-start.2
  165.8 2.3 %copy.17 = bf16[256,2048]{1,0:T(8,128)(2,1)} copy(bf16[256,2048]{1,0:T(8,128)(2,1)} %get-tuple-element.20) | data formatting | bytes 2097152
  168.2 0.0 copy-done.3
  168.2 0.6 copy.18
  168.8 0.0 copy-done.2
  168.8 0.0 copy-start.1
  168.8 0.7 copy.19
  169.5 0.3 copy-done.1
  169.8 0.0 copy-start
  169.8 0.7 copy.20
  170.5 0.3 copy-done
  170.8 0.7 copy.21
Async XLA Ops:
  165.8 2.4 %copy-start.3 = (bf16[8,256]{1,0:T(8,128)(2,1)S(1)}, bf16[8,256]{1,0:T(8,128)(2,1)}, u32[]{:S(2)}) copy-start(bf16[8,256]{1,0:T(8,128)(2,1)} %get-tuple-element.11) | copy-start | bytes 12292
  165.8 3.0 %copy-start.2 = (bf16[128,768]{1,0:T(8,128)(2,1)S(1)}, bf16[128,768]{1,0:T(8,128)(2,1)}, u32[]{:S(2)}) copy-start(bf16[128,768]{1,0:T(8,128)(2,1)} %get-tuple-element.12) | copy-start | bytes 589828
  168.8 1.0 copy-start.1
  169.8 1.0 copy-start

commit v3 on v2

--- a/solution.py
+++ b/solution.py
@@ -35,10 +35,10 @@
 
 
 def kernel(
-    tok, og, ids_t, gp_t, wg, wu, wd,
+    tok_in, og_in, ids_t, gp_t, wg, wu, wd,
     in_grad, gate_grad, gg, gu, gd,
-    w, snd, rcv, xt, qt, dl, hh, cs, cr, tb, sb, rf, ry, xs, rx, pm, ptm, gc,
-    w_ss, w_rs, a_ss, a_rs, c_ss, c_rs, s_ss, s_rs, f_ss, f_rs, y_ss, y_rs, x_ss, x_rs,
+    tok, og, w, snd, rcv, xt, qt, dl, hh, cs, cr, tb, sb, rf, ry, xs, rx, pm, ptm, gc,
+    w_ss, w_rs, a_ss, a_rs, c_ss, c_rs, s_ss, s_rs, f_ss, f_rs, y_ss, y_rs, x_ss, x_rs, l_s,
 ):
     f = lax.axis_index("fsdp")
     e = lax.axis_index("ep")
@@ -67,16 +67,23 @@
     def wrows(fs):
         return w.at[pl.ds(pl.multiple_of(fs * SHARD, SHARD), SHARD), :]
 
+    own = pl.ds(pl.multiple_of(f * SHARD, SHARD), SHARD)
+    loads = [
+        pltpu.make_async_copy(tok_in, tok, l_s.at[0]),
+        pltpu.make_async_copy(og_in, og, l_s.at[1]),
+        pltpu.make_async_copy(wg, w.at[own, 0:FF], l_s.at[2]),
+        pltpu.make_async_copy(wu, w.at[own, FF:2 * FF], l_s.at[3]),
+        pltpu.make_async_copy(wd, w.at[own, 2 * FF:], l_s.at[4]),
+    ]
+    for cp in loads:
+        cp.start()
+
     barrier = pltpu.get_barrier_semaphore()
     peers = [(f, owner(i, 1)) for i in range(1, N_EP)]
     peers += [fdev(1, 0, 0), fdev(0, 1, 0), fdev(0, 2, 0), fdev(0, 3, 0), fdev(0, 0, 1)]
     for dev in peers:
         pl.semaphore_signal(barrier, inc=1, device_id=dev, device_id_type=MESH)
 
-    own = pl.ds(pl.multiple_of(f * SHARD, SHARD), SHARD)
-    w[own, 0:FF] = wg[...]
-    w[own, FF:2 * FF] = wu[...]
-    w[own, 2 * FF:] = wd[...]
 
     idt = ids_t[...]
     gpt = gp_t[...].astype(F32)
@@ -99,14 +106,7 @@
         gcol = jnp.sum(jnp.where(hit, gates[i], 0.0), axis=1, keepdims=True)
         gc[i * MOST:(i + 1) * MOST, :] = jnp.broadcast_to(gcol, (MOST, 128))
 
-    pl.semaphore_wait(barrier, len(peers))
-
-    send(wrows(f), wrows(f), w_ss.at[0], w_rs.at[0], fdev(1, 0, 0))
-    for d in (1, 2, 3):
-        send(wrows(f), wrows(f), w_ss.at[d], w_rs.at[d], fdev(0, d, 0))
-    send(wrows(f), wrows(f), w_ss.at[7], w_rs.at[7], fdev(0, 0, 1))
-
-    for half in (0, 1):
+    def gather(half):
         rows = slice(half * 256, half * 256 + 256)
         pick = pm[rows, :]
         gcol = gc[rows, 0:1]
@@ -116,16 +116,32 @@
             snd[rows, D + n * 512:D + n * 512 + 512] = (
                 gcol * dot(pick, og[:, cols])
             ).astype(BF)
+
+    def dispatch(half):
         for i in range(half * 8, half * 8 + 8):
             part = pl.ds(i * MOST, MOST)
-            if i == 0:
-                rcv[part, :] = snd[part, :]
-            else:
+            if i:
                 send(
                     snd.at[part, :], rcv.at[part, :], a_ss.at[i - 1], a_rs.at[i - 1],
                     (f, owner(i, 1)),
                 )
-        ptm[:, rows] = pick.T
+
+    for cp in loads:
+        cp.wait()
+    gather(0)
+    pl.semaphore_wait(barrier, len(peers))
+
+    send(wrows(f), wrows(f), w_ss.at[0], w_rs.at[0], fdev(1, 0, 0))
+    for d in (1, 2, 3):
+        send(wrows(f), wrows(f), w_ss.at[d], w_rs.at[d], fdev(0, d, 0))
+    send(wrows(f), wrows(f), w_ss.at[7], w_rs.at[7], fdev(0, 0, 1))
+
+    dispatch(0)
+    gather(1)
+    dispatch(1)
+    rcv[0:MOST, :] = snd[0:MOST, :]
+    for half in (0, 1):
+        ptm[:, half * 256:half * 256 + 256] = pm[half * 256:half * 256 + 256, :].T
 
     def arrived(k, fs):
         copy(wrows(fs), wrows(fs), w_ss.at[0], w_rs.at[k], fdev(0, 0, 1)).wait_recv()
@@ -147,16 +163,11 @@
         for d in (1, 2, 3):
             arrived(8 + base + d, fdev(dx, 4 - d, 1)[0])
 
-    for first, count in BLOCKS:
-        for i in range(first, first + count):
-            if i:
-                part = pl.ds(i * MOST, MOST)
-                copy(
-                    snd.at[part, :], rcv.at[part, :], a_ss.at[i - 1], a_rs.at[i - 1],
-                    (f, owner(i, 1)),
-                ).wait_recv()
-        n_rows = count * MOST
-        rows = slice(first * MOST, first * MOST + n_rows)
+    def block_rows(first, count):
+        return slice(first * MOST, (first + count) * MOST)
+
+    def forward(first, count):
+        rows = block_rows(first, count)
         xt[:, rows] = rcv[rows, 0:D].T
         qt[:, rows] = rcv[rows, D:].T
 
@@ -174,8 +185,13 @@
             dl[rows, pl.ds(at + FF, 256)] = (r * silu).astype(BF)
             return pick_sum + jnp.sum(h.astype(F32) * r, axis=1, keepdims=True)
 
-        pick_sum = lax.fori_loop(0, FF // 256, hidden, jnp.zeros((n_rows, 1), F32))
-        cs[rows, D:] = jnp.broadcast_to(pick_sum, (n_rows, 128)).astype(BF)
+        pick_sum = lax.fori_loop(
+            0, FF // 256, hidden, jnp.zeros((count * MOST, 1), F32)
+        )
+        cs[rows, D:] = jnp.broadcast_to(pick_sum, (count * MOST, 128)).astype(BF)
+
+    def backward(first, count):
+        rows = block_rows(first, count)
 
         def back(m, carry):
             at = pl.multiple_of(m * 256, 256)
@@ -186,6 +202,8 @@
             return carry
 
         lax.fori_loop(0, D // 256, back, 0)
+
+    def give_back(first, count):
         for i in range(first, first + count):
             part = pl.ds(i * MOST, MOST)
             if i == 0:
@@ -195,6 +213,22 @@
                     cs.at[part, :], cr.at[part, :], c_ss.at[i - 1], c_rs.at[i - 1],
                     (f, owner(i, -1)),
                 )
+
+    last = BLOCKS[-1]
+    for block in BLOCKS:
+        for i in range(block[0], block[0] + block[1]):
+            if i:
+                part = pl.ds(i * MOST, MOST)
+                copy(
+                    snd.at[part, :], rcv.at[part, :], a_ss.at[i - 1], a_rs.at[i - 1],
+                    (f, owner(i, 1)),
+                ).wait_recv()
+        if block is last:
+            for earlier in BLOCKS[:-1]:
+                give_back(*earlier)
+        forward(*block)
+        if block is not last:
+            backward(*block)
 
     mine, other = pl.multiple_of(c * SHARD, SHARD), pl.multiple_of((1 - c) * SHARD, SHARD)
 
@@ -234,6 +268,8 @@
         )
         if j in (1, 2):
             reduce_pair(j - 1)
+    backward(*last)
+    give_back(*last)
     for j in range(2, len(CHIPS)):
         reduce_pair(j)
 
@@ -259,7 +295,9 @@
         cr[part, D:] = jnp.where(lane == owner(i, 1), cr[part, D:], jnp.zeros((), BF))
     for n in range(4):
         cols = slice(n * 512, n * 512 + 512)
-        in_grad[:, cols] = dot(ptm[...], cr[:, cols]).astype(BF)
+        tok[:, cols] = dot(ptm[...], cr[:, cols]).astype(BF)
+    store = pltpu.make_async_copy(tok, in_grad, l_s.at[5])
+    store.start()
     picks = dot(ptm[...], cr[:, D:]).T
     got = jnp.zeros((8, TOK), F32)
     for expert in range(N_EP):
@@ -272,12 +310,14 @@
     gg[...] = total[:, 0:FF]
     gu[...] = total[:, FF:2 * FF]
     gd[...] = total[:, 2 * FF:]
+    store.wait()
     for cp in sends:
         cp.wait_send()
 
 
 def per_device(tokens, out_grad, expert_ids, gate_probs, w_gate, w_up, w_down):
     vmem = pl.BlockSpec(memory_space=pltpu.VMEM)
+    hbm = pl.BlockSpec(memory_space=pl.ANY)
     dma = pltpu.SemaphoreType.DMA
     outs = pl.pallas_call(
         kernel,
@@ -285,9 +325,11 @@
             jax.ShapeDtypeStruct((TOK, D), BF),
             jax.ShapeDtypeStruct((8, TOK), BF),
         ) + (jax.ShapeDtypeStruct((SHARD, FF), BF),) * 3,
-        in_specs=[vmem] * 7,
-        out_specs=(vmem,) * 5,
+        in_specs=[hbm, hbm, vmem, vmem, hbm, hbm, hbm],
+        out_specs=(hbm,) + (vmem,) * 4,
         scratch_shapes=[
+            pltpu.VMEM((TOK, D), BF),
+            pltpu.VMEM((TOK, D), BF),
             pltpu.VMEM((D, 3 * FF), BF),
             pltpu.VMEM((ROWS, 2 * D), BF),
             pltpu.VMEM((ROWS, 2 * D), BF),
@@ -307,7 +349,7 @@
             pltpu.VMEM((TOK, ROWS), BF),
             pltpu.VMEM((ROWS, 128), F32),
             dma((15,)), dma((15,)), dma((15,)), dma((15,)), dma((15,)), dma((15,)),
-            dma((8,)), dma((8,)), dma((4,)), dma((4,)), dma((4,)), dma((4,)), dma, dma,
+            dma((8,)), dma((8,)), dma((4,)), dma((4,)), dma((4,)), dma((4,)), dma, dma, dma((6,)),
         ],
         compiler_params=pltpu.CompilerParams(
             collective_id=0, has_side_effects=True, vmem_limit_bytes=62 * 2**20

time: 172 us -> 168 us (0.977)
  Pallas kernels: 165 us -> 161 us
    pallas_call x1, Pallas kernels: 165 us -> 161 us  [per_device(): pl.pallas_call(kernel, out_shape=(jax.ShapeDtypeStruct((TOK, D), BF), jax...]
where the time goes in v3:
time: 168 us; the launch traced here: 167 us
  Pallas kernels  161 us (96%)
  local copies, waits for them, and re-layouts  5.61 us (3%)
    pallas_call x1, Pallas kernels, per_device(): pl.pallas_call(kernel, out_shape=(jax.ShapeDtypeStruct((TOK, D), BF), jax...  161 us
    unnamed x13, local copies, waits for them, and re-layouts  5.61 us

profile of v3, /device:TPU:33, one launch (start us, length us, event | category | flops | bytes accessed | tf_op | source)
XLA Modules:
  0.0 167.4 jit_solution(11306330057891717351)
XLA Ops:
  0.6 161.1 %expert_backward.1 = (bf16[256,2048]{1,0:T(8,128)(2,1)}, bf16[8,256]{1,0:T(8,128)(2,1)}, bf16[128,768]{1,0:T(8,128)(2,1)}, bf16[128,768]{1,0:T(8,128)(2,1)}, bf16[128,768]{1,0:T(8,128)(2,1)}) custom-call(bf16[256,2048]{1,0:T(8,128)(2,1)} %tok_in.1, bf16[256,2048]{1,0:T(8,128)(2,1)} %og_in.1, s32[8,256]{1,0:T(8,128)} %bitcast.15, bf16[8,256]{1,0:T(8,128)(2,1)} %bitcast.16, ...), custom_call_target="tpu_custom_call" | custom-call | tf_op jit(solution)/shard_map/expert_backward/pallas_call | solution.py:322
  161.7 0.0 copy-start.3
  161.7 0.0 copy-start.2
  161.7 2.3 %copy.17 = bf16[256,2048]{1,0:T(8,128)(2,1)} copy(bf16[256,2048]{1,0:T(8,128)(2,1)} %get-tuple-element.20) | data formatting | bytes 2097152
  164.1 0.0 copy-done.3
  164.1 0.6 copy.18
  164.7 0.0 copy-done.2
  164.7 0.0 copy-start.1
  164.7 0.7 copy.19
  165.4 0.3 copy-done.1
  165.7 0.0 copy-start
  165.7 0.7 copy.20
  166.4 0.3 copy-done
  166.7 0.7 copy.21
Async XLA Ops:
  161.7 2.4 %copy-start.3 = (bf16[8,256]{1,0:T(8,128)(2,1)S(1)}, bf16[8,256]{1,0:T(8,128)(2,1)}, u32[]{:S(2)}) copy-start(bf16[8,256]{1,0:T(8,128)(2,1)} %get-tuple-element.11) | copy-start | bytes 12292
  161.7 3.0 %copy-start.2 = (bf16[128,768]{1,0:T(8,128)(2,1)S(1)}, bf16[128,768]{1,0:T(8,128)(2,1)}, u32[]{:S(2)}) copy-start(bf16[128,768]{1,0:T(8,128)(2,1)} %get-tuple-element.12) | copy-start | bytes 589828
  164.7 1.0 copy-start.1
  165.7 1.0 copy-start

commit v4 on v3

--- a/solution.py
+++ b/solution.py
@@ -18,7 +18,6 @@
 ROWS = N_EP * MOST
 SHARD = 128
 HALF = SHARD // 2
-CW = D + 128
 
 OFFS = (
     (0, 0), (1, 0), (0, 1), (0, 7),
@@ -36,9 +35,9 @@
 
 def kernel(
     tok_in, og_in, ids_t, gp_t, wg, wu, wd,
-    in_grad, gate_grad, gg, gu, gd,
-    tok, og, w, snd, rcv, xt, qt, dl, hh, cs, cr, tb, sb, rf, ry, xs, rx, pm, ptm, gc,
-    w_ss, w_rs, a_ss, a_rs, c_ss, c_rs, s_ss, s_rs, f_ss, f_rs, y_ss, y_rs, x_ss, x_rs, l_s,
+    in_grad, gate_grad, grads,
+    tok, og, w, snd, rcv, xt, qt, dl, hh, cs, cr, ps, pr, pv, tb, sb, rf, ry, xs, rx, pm, ptm, gc,
+    w_ss, w_rs, a_ss, a_rs, c_ss, c_rs, p_ss, p_rs, s_ss, s_rs, f_ss, f_rs, y_ss, y_rs, x_ss, x_rs, l_s,
 ):
     f = lax.axis_index("fsdp")
     e = lax.axis_index("ep")
@@ -168,11 +167,12 @@
 
     def forward(first, count):
         rows = block_rows(first, count)
-        xt[:, rows] = rcv[rows, 0:D].T
-        qt[:, rows] = rcv[rows, D:].T
 
         def hidden(n, pick_sum):
             at = pl.multiple_of(n * 256, 256)
+            third = pl.multiple_of(n * 640, 128)
+            xt[pl.ds(third, FF), rows] = rcv[rows, pl.ds(third, FF)].T
+            qt[pl.ds(third, FF), rows] = rcv[rows, pl.ds(D + third, FF)].T
             x = rcv[rows, 0:D]
             a = dot(x, w[:, pl.ds(at, 256)])
             b = dot(x, w[:, pl.ds(at + FF, 256)])
@@ -188,7 +188,7 @@
         pick_sum = lax.fori_loop(
             0, FF // 256, hidden, jnp.zeros((count * MOST, 1), F32)
         )
-        cs[rows, D:] = jnp.broadcast_to(pick_sum, (count * MOST, 128)).astype(BF)
+        ps[:, rows] = jnp.broadcast_to(pick_sum, (count * MOST, 128)).T[0:16, :].astype(BF)
 
     def backward(first, count):
         rows = block_rows(first, count)
@@ -206,13 +206,14 @@
     def give_back(first, count):
         for i in range(first, first + count):
             part = pl.ds(i * MOST, MOST)
+            four = pl.ds(i // 4 * 128, 128)
             if i == 0:
                 cr[part, :] = cs[part, :]
+                pr[0] = ps[:, four]
             else:
-                send(
-                    cs.at[part, :], cr.at[part, :], c_ss.at[i - 1], c_rs.at[i - 1],
-                    (f, owner(i, -1)),
-                )
+                dev = (f, owner(i, -1))
+                send(cs.at[part, :], cr.at[part, :], c_ss.at[i - 1], c_rs.at[i - 1], dev)
+                send(ps.at[:, four], pr.at[i], p_ss.at[i - 1], p_rs.at[i - 1], dev)
 
     last = BLOCKS[-1]
     for block in BLOCKS:
@@ -224,8 +225,7 @@
                     (f, owner(i, 1)),
                 ).wait_recv()
         if block is last:
-            for earlier in BLOCKS[:-1]:
-                give_back(*earlier)
+            give_back(*BLOCKS[0])
         forward(*block)
         if block is not last:
             backward(*block)
@@ -268,6 +268,8 @@
         )
         if j in (1, 2):
             reduce_pair(j - 1)
+            if j == 1:
+                give_back(*BLOCKS[1])
     backward(*last)
     give_back(*last)
     for j in range(2, len(CHIPS)):
@@ -284,35 +286,61 @@
     xs[...] = y_sum(1).astype(BF)
     send(xs, rx, x_ss, x_rs, fdev(1, 0, 0))
 
-    lane = lax.broadcasted_iota(jnp.int32, (MOST, 128), 1)
+    lane = lax.broadcasted_iota(jnp.int32, (1, ROWS), 1)
     for i in range(N_EP):
         part = pl.ds(i * MOST, MOST)
+        four = pl.ds(i // 4 * 128, 128)
         if i:
+            dev = (f, owner(i, -1))
             copy(
-                cs.at[part, :], cr.at[part, :], c_ss.at[i - 1], c_rs.at[i - 1],
-                (f, owner(i, -1)),
+                cs.at[part, :], cr.at[part, :], c_ss.at[i - 1], c_rs.at[i - 1], dev
             ).wait_recv()
-        cr[part, D:] = jnp.where(lane == owner(i, 1), cr[part, D:], jnp.zeros((), BF))
+            copy(ps.at[:, four], pr.at[i], p_ss.at[i - 1], p_rs.at[i - 1], dev).wait_recv()
+        row = jnp.concatenate([pr[i, 0:1, :].astype(F32)] * 4, axis=1)
+        pv[i:i + 1, :] = jnp.where(lane // MOST == i, row, 0.0)
     for n in range(4):
         cols = slice(n * 512, n * 512 + 512)
         tok[:, cols] = dot(ptm[...], cr[:, cols]).astype(BF)
     store = pltpu.make_async_copy(tok, in_grad, l_s.at[5])
     store.start()
-    picks = dot(ptm[...], cr[:, D:]).T
+    picks = dot(pv[...].astype(BF), pm[...])
     got = jnp.zeros((8, TOK), F32)
-    for expert in range(N_EP):
-        got = got + jnp.where(idt == expert, picks[expert:expert + 1, :], 0.0)
+    for i in range(N_EP):
+        got = got + jnp.where(idt == owner(i, 1), picks[i:i + 1, :], 0.0)
     gate_grad[...] = (got / gpt).astype(BF)
 
     total = y_sum(0)
     copy(xs, rx, x_ss, x_rs, fdev(1, 0, 0)).wait_recv()
     total = (total + rx[...].astype(F32)).astype(BF)
-    gg[...] = total[:, 0:FF]
-    gu[...] = total[:, FF:2 * FF]
-    gd[...] = total[:, 2 * FF:]
+    grads[...] = total
     store.wait()
     for cp in sends:
         cp.wait_send()
+
+
+def hand_over(
+    in_grad, gate_grad, grads, in_out, gate_out, gg, gu, gd, in_buf, gate_buf, g_buf,
+    load_sems, store_sems,
+):
+    loads = [(in_grad.at[n * 64:n * 64 + 64, :], in_buf.at[n * 64:n * 64 + 64, :]) for n in range(4)]
+    loads += [(grads.at[:, n * FF:(n + 1) * FF], g_buf.at[n]) for n in range(3)]
+    loads += [(gate_grad, gate_buf)]
+    stores = [(in_buf.at[n * 64:n * 64 + 64, :], in_out.at[n * 64:n * 64 + 64, :]) for n in range(4)]
+    stores += [(g_buf.at[n], g) for n, g in enumerate((gg, gu, gd))]
+    stores += [(gate_buf, gate_out)]
+    loads = [
+        pltpu.make_async_copy(src, dst, load_sems.at[n]) for n, (src, dst) in enumerate(loads)
+    ]
+    stores = [
+        pltpu.make_async_copy(src, dst, store_sems.at[n]) for n, (src, dst) in enumerate(stores)
+    ]
+    for cp in loads:
+        cp.start()
+    for load, store in zip(loads, stores):
+        load.wait()
+        store.start()
+    for cp in stores:
+        cp.wait()
 
 
 def per_device(tokens, out_grad, expert_ids, gate_probs, w_gate, w_up, w_down):
@@ -324,9 +352,10 @@
         out_shape=(
             jax.ShapeDtypeStruct((TOK, D), BF),
             jax.ShapeDtypeStruct((8, TOK), BF),
-        ) + (jax.ShapeDtypeStruct((SHARD, FF), BF),) * 3,
+            jax.ShapeDtypeStruct((SHARD, 3 * FF), BF),
+        ),
         in_specs=[hbm, hbm, vmem, vmem, hbm, hbm, hbm],
-        out_specs=(hbm,) + (vmem,) * 4,
+        out_specs=(hbm, vmem, vmem),
         scratch_shapes=[
             pltpu.VMEM((TOK, D), BF),
             pltpu.VMEM((TOK, D), BF),
@@ -337,8 +366,11 @@
             pltpu.VMEM((D, ROWS), BF),
             pltpu.VMEM((ROWS, 2 * FF), BF),
             pltpu.VMEM((ROWS, FF), BF),
-            pltpu.VMEM((ROWS, CW), BF),
-            pltpu.VMEM((ROWS, CW), BF),
+            pltpu.VMEM((ROWS, D), BF),
+            pltpu.VMEM((ROWS, D), BF),
+            pltpu.VMEM((16, ROWS), BF),
+            pltpu.VMEM((N_EP, 16, 128), BF),
+            pltpu.VMEM((N_EP, ROWS), F32),
             pltpu.VMEM((8, 256, 3 * FF), BF),
             pltpu.VMEM((8 * SHARD, 3 * FF), BF),
             pltpu.VMEM((4, HALF, 3 * FF), BF),
@@ -349,6 +381,7 @@
             pltpu.VMEM((TOK, ROWS), BF),
             pltpu.VMEM((ROWS, 128), F32),
             dma((15,)), dma((15,)), dma((15,)), dma((15,)), dma((15,)), dma((15,)),
+            dma((15,)), dma((15,)),
             dma((8,)), dma((8,)), dma((4,)), dma((4,)), dma((4,)), dma((4,)), dma, dma, dma((6,)),
         ],
         compiler_params=pltpu.CompilerParams(
@@ -359,7 +392,23 @@
         tokens, out_grad, expert_ids.T, gate_probs.T,
         w_gate[:, 0, :], w_up[:, 0, :], w_down[:, 0, :],
     )
-    in_grad, gate_grad, g_gate, g_up, g_down = outs
+    finish = pl.pallas_call(
+        hand_over,
+        out_shape=(
+            jax.ShapeDtypeStruct((TOK, D), BF),
+            jax.ShapeDtypeStruct((8, TOK), BF),
+        ) + (jax.ShapeDtypeStruct((SHARD, FF), BF),) * 3,
+        in_specs=[hbm] * 3,
+        out_specs=(hbm,) * 5,
+        scratch_shapes=[
+            pltpu.VMEM((TOK, D), BF),
+            pltpu.VMEM((8, TOK), BF),
+            pltpu.VMEM((3, SHARD, FF), BF),
+            dma((8,)), dma((8,)),
+        ],
+        name="hand_over",
+    )
+    in_grad, gate_grad, g_gate, g_up, g_down = finish(*outs)
     return in_grad, gate_grad.T, g_gate[:, None, :], g_up[:, None, :], g_down[:, None, :]
 
 

time: 168 us -> 164 us (0.976)
  local copies, waits for them, and re-layouts: 5.61 us -> 0 us
  Pallas kernels: 161 us -> 163 us
    unnamed x13 -> x0, local copies, waits for them, and re-layouts: 5.61 us -> none
    pallas_call x0 -> x1, Pallas kernels: none -> 2.24 us  [per_device(): in_grad, gate_grad, g_gate, g_up, g_down = finish(*outs)]
where the time goes in v4:
time: 164 us
  Pallas kernels  163 us (99%)
    pallas_call x1, Pallas kernels, per_device(): pl.pallas_call(kernel, out_shape=(jax.ShapeDtypeStruct((TOK, D), BF), jax...  161 us

profile of v4, /device:TPU:33, one launch (start us, length us, event | category | flops | bytes accessed | tf_op | source)
XLA Modules:
  0.0 163.8 jit_solution(9285122723124618543)
XLA Ops:
  0.6 160.7 %expert_backward.1 = (bf16[256,2048]{1,0:T(8,128)(2,1)}, bf16[8,256]{1,0:T(8,128)(2,1)}, bf16[128,2304]{1,0:T(8,128)(2,1)}) custom-call(bf16[256,2048]{1,0:T(8,128)(2,1)} %tok_in.1, bf16[256,2048]{1,0:T(8,128)(2,1)} %og_in.1, s32[8,256]{1,0:T(8,128)} %bitcast.12, bf16[8,256]{1,0:T(8,128)(2,1)} %bitcast.13, bf16[128,768]{1,0:T(8,128)(2,1)} %bitcast.9, ...), custom_call_target="tpu_custom_call" | custom-call | tf_op jit(solution)/shard_map/expert_backward/pallas_call | solution.py:350
  161.4 2.2 %hand_over.1 = (bf16[256,2048]{1,0:T(8,128)(2,1)}, bf16[8,256]{1,0:T(8,128)(2,1)}, bf16[128,768]{1,0:T(8,128)(2,1)}, bf16[128,768]{1,0:T(8,128)(2,1)}, bf16[128,768]{1,0:T(8,128)(2,1)}) custom-call(bf16[256,2048]{1,0:T(8,128)(2,1)} %get-tuple-element.13.in_grad, bf16[8,256]{1,0:T(8,128)(2,1)} %get-tuple-element.14.gate_grad, ...), custom_call_target="tpu_custom_call" | custom-call | tf_op jit(solution)/shard_map/hand_over/pallas_call | solution.py:411

commit v5 on v4

--- a/solution.py
+++ b/solution.py
@@ -23,11 +23,13 @@
     (0, 0), (1, 0), (0, 1), (0, 7),
     (1, 1), (1, 7), (0, 2), (0, 6),
     (1, 2), (1, 6), (0, 3), (0, 5),
-    (1, 3), (1, 5), (0, 4), (1, 4),
+    (1, 5), (1, 3), (1, 4), (0, 4),
 )
 BLOCKS = ((0, 8), (8, 4), (12, 4))
 CHIPS = ((1, 2), (0, 2), (1, 1), (1, 3), (0, 1), (0, 3), (1, 0), (0, 0))
 
+AFTER = ((), (0,), (1,), (), (2,), (3,), (4, 5), (6, 7))
+
 
 def dot(a, b):
     return jnp.dot(a, b, preferred_element_type=F32)
@@ -36,7 +38,7 @@
 def kernel(
     tok_in, og_in, ids_t, gp_t, wg, wu, wd,
     in_grad, gate_grad, grads,
-    tok, og, w, snd, rcv, xt, qt, dl, hh, cs, cr, ps, pr, pv, tb, sb, rf, ry, xs, rx, pm, ptm, gc,
+    tok, og, w, wt, snd, rcv, xt, qt, dl, hh, cs, cr, ps, pr, pv, tb, sb, rf, ry, xs, rx, pm, ptm, gc,
     w_ss, w_rs, a_ss, a_rs, c_ss, c_rs, p_ss, p_rs, s_ss, s_rs, f_ss, f_rs, y_ss, y_rs, x_ss, x_rs, l_s,
 ):
     f = lax.axis_index("fsdp")
@@ -142,6 +144,12 @@
     for half in (0, 1):
         ptm[:, half * 256:half * 256 + 256] = pm[half * 256:half * 256 + 256, :].T
 
+    def turn(fs):
+        at = pl.multiple_of(fs * SHARD, SHARD)
+        wt[:, pl.ds(at, SHARD)] = w[pl.ds(at, SHARD), 0:2 * FF].T
+
+    turn(f)
+
     def arrived(k, fs):
         copy(wrows(fs), wrows(fs), w_ss.at[0], w_rs.at[k], fdev(0, 0, 1)).wait_recv()
 
@@ -150,17 +158,23 @@
     for d in (1, 2, 3):
         send(wrows(far), wrows(far), w_ss.at[3 + d], w_rs.at[3 + d], fdev(0, d, 0))
     send(wrows(far), wrows(far), w_ss.at[8], w_rs.at[8], fdev(0, 0, 1))
+    turn(far)
     for dx, base in ((0, 0), (1, 3)):
         for d in (1, 2, 3):
             fs = fdev(dx, 4 - d, 0)[0]
             arrived(base + d, fs)
             k = 8 + base + d
             send(wrows(fs), wrows(fs), w_ss.at[k], w_rs.at[k], fdev(0, 0, 1))
-    arrived(7, fdev(0, 0, 1)[0])
-    arrived(8, fdev(1, 0, 1)[0])
+            turn(fs)
+    for k in (0, 1):
+        fs = fdev(k, 0, 1)[0]
+        arrived(7 + k, fs)
+        turn(fs)
     for dx, base in ((0, 0), (1, 3)):
         for d in (1, 2, 3):
-            arrived(8 + base + d, fdev(dx, 4 - d, 1)[0])
+            fs = fdev(dx, 4 - d, 1)[0]
+            arrived(8 + base + d, fs)
+            turn(fs)
 
     def block_rows(first, count):
         return slice(first * MOST, (first + count) * MOST)
@@ -195,10 +209,7 @@
 
         def back(m, carry):
             at = pl.multiple_of(m * 256, 256)
-            cs[rows, pl.ds(at, 256)] = lax.dot_general(
-                dl[rows, :], w[pl.ds(at, 256), 0:2 * FF], (((1,), (1,)), ((), ())),
-                preferred_element_type=F32,
-            ).astype(BF)
+            cs[rows, pl.ds(at, 256)] = dot(dl[rows, :], wt[:, pl.ds(at, 256)]).astype(BF)
             return carry
 
         lax.fori_loop(0, D // 256, back, 0)
@@ -206,14 +217,20 @@
     def give_back(first, count):
         for i in range(first, first + count):
             part = pl.ds(i * MOST, MOST)
-            four = pl.ds(i // 4 * 128, 128)
             if i == 0:
                 cr[part, :] = cs[part, :]
-                pr[0] = ps[:, four]
             else:
                 dev = (f, owner(i, -1))
                 send(cs.at[part, :], cr.at[part, :], c_ss.at[i - 1], c_rs.at[i - 1], dev)
-                send(ps.at[:, four], pr.at[i], p_ss.at[i - 1], p_rs.at[i - 1], dev)
+
+    def give_picks_back():
+        pr[0] = ps[:, 0:128]
+        for i in range(1, N_EP):
+            four = pl.ds(i // 4 * 128, 128)
+            send(
+                ps.at[:, four], pr.at[i], p_ss.at[i - 1], p_rs.at[i - 1],
+                (f, owner(i, -1)),
+            )
 
     last = BLOCKS[-1]
     for block in BLOCKS:
@@ -225,7 +242,8 @@
                     (f, owner(i, 1)),
                 ).wait_recv()
         if block is last:
-            give_back(*BLOCKS[0])
+            for earlier in BLOCKS[:-1]:
+                give_back(*earlier)
         forward(*block)
         if block is not last:
             backward(*block)
@@ -266,14 +284,12 @@
             tb.at[j, pl.ds(other, SHARD), :], sb.at[pl.ds(j * SHARD, SHARD), :],
             s_ss.at[j], s_rs.at[j], fdev(0, 0, 1),
         )
-        if j in (1, 2):
-            reduce_pair(j - 1)
-            if j == 1:
-                give_back(*BLOCKS[1])
-    backward(*last)
-    give_back(*last)
-    for j in range(2, len(CHIPS)):
-        reduce_pair(j)
+        for ready in AFTER[j]:
+            reduce_pair(ready)
+        if j == 3:
+            backward(*last)
+            give_back(*last)
+            give_picks_back()
 
     def y_sum(dx):
         j = CHIPS.index((dx, 0))
@@ -360,6 +376,7 @@
             pltpu.VMEM((TOK, D), BF),
             pltpu.VMEM((TOK, D), BF),
             pltpu.VMEM((D, 3 * FF), BF),
+            pltpu.VMEM((2 * FF, D), BF),
             pltpu.VMEM((ROWS, 2 * D), BF),
             pltpu.VMEM((ROWS, 2 * D), BF),
             pltpu.VMEM((D, ROWS), BF),

time: 164 us -> 162 us (0.988)
  Pallas kernels: 163 us -> 161 us
    pallas_call x1, Pallas kernels: 161 us -> 159 us  [per_device(): pl.pallas_call(kernel, out_shape=(jax.ShapeDtypeStruct((TOK, D), BF), jax...]
where the time goes in v5:
time: 162 us
  Pallas kernels  161 us (99%)
    pallas_call x1, Pallas kernels, per_device(): pl.pallas_call(kernel, out_shape=(jax.ShapeDtypeStruct((TOK, D), BF), jax...  159 us

profile of v5, /device:TPU:33, one launch (start us, length us, event | category | flops | bytes accessed | tf_op | source)
XLA Modules:
  0.0 162.1 jit_solution(9612858475110353573)
XLA Ops:
  0.6 159.1 %expert_backward.1 = (bf16[256,2048]{1,0:T(8,128)(2,1)}, bf16[8,256]{1,0:T(8,128)(2,1)}, bf16[128,2304]{1,0:T(8,128)(2,1)}) custom-call(bf16[256,2048]{1,0:T(8,128)(2,1)} %tok_in.1, bf16[256,2048]{1,0:T(8,128)(2,1)} %og_in.1, s32[8,256]{1,0:T(8,128)} %bitcast.12, bf16[8,256]{1,0:T(8,128)(2,1)} %bitcast.13, bf16[128,768]{1,0:T(8,128)(2,1)} %bitcast.9, ...), custom_call_target="tpu_custom_call" | custom-call | tf_op jit(solution)/shard_map/expert_backward/pallas_call | solution.py:366
  159.7 2.2 %hand_over.1 = (bf16[256,2048]{1,0:T(8,128)(2,1)}, bf16[8,256]{1,0:T(8,128)(2,1)}, bf16[128,768]{1,0:T(8,128)(2,1)}, bf16[128,768]{1,0:T(8,128)(2,1)}, bf16[128,768]{1,0:T(8,128)(2,1)}) custom-call(bf16[256,2048]{1,0:T(8,128)(2,1)} %get-tuple-element.13.in_grad, bf16[8,256]{1,0:T(8,128)(2,1)} %get-tuple-element.14.gate_grad, ...), custom_call_target="tpu_custom_call" | custom-call | tf_op jit(solution)/shard_map/hand_over/pallas_call | solution.py:428

commit v6 on v5

--- a/solution.py
+++ b/solution.py
@@ -22,7 +22,7 @@
 OFFS = (
     (0, 0), (1, 0), (0, 1), (0, 7),
     (1, 1), (1, 7), (0, 2), (0, 6),
-    (1, 2), (1, 6), (0, 3), (0, 5),
+    (1, 6), (1, 2), (0, 5), (0, 3),
     (1, 5), (1, 3), (1, 4), (0, 4),
 )
 BLOCKS = ((0, 8), (8, 4), (12, 4))

time: 162 us -> 162 us (level)
  no operation moved by 1% of the time
where the time goes in v6:
time: 162 us
  Pallas kernels  161 us (99%)
    pallas_call x1, Pallas kernels, per_device(): pl.pallas_call(kernel, out_shape=(jax.ShapeDtypeStruct((TOK, D), BF), jax...  159 us

profile of v6, /device:TPU:33, one launch (start us, length us, event | category | flops | bytes accessed | tf_op | source)
XLA Modules:
  0.0 162.1 jit_solution(12616874615502868055)
XLA Ops:
  0.6 159.1 %expert_backward.1 = (bf16[256,2048]{1,0:T(8,128)(2,1)}, bf16[8,256]{1,0:T(8,128)(2,1)}, bf16[128,2304]{1,0:T(8,128)(2,1)}) custom-call(bf16[256,2048]{1,0:T(8,128)(2,1)} %tok_in.1, bf16[256,2048]{1,0:T(8,128)(2,1)} %og_in.1, s32[8,256]{1,0:T(8,128)} %bitcast.12, bf16[8,256]{1,0:T(8,128)(2,1)} %bitcast.13, bf16[128,768]{1,0:T(8,128)(2,1)} %bitcast.9, ...), custom_call_target="tpu_custom_call" | custom-call | tf_op jit(solution)/shard_map/expert_backward/pallas_call | solution.py:366
  159.7 2.2 %hand_over.1 = (bf16[256,2048]{1,0:T(8,128)(2,1)}, bf16[8,256]{1,0:T(8,128)(2,1)}, bf16[128,768]{1,0:T(8,128)(2,1)}, bf16[128,768]{1,0:T(8,128)(2,1)}, bf16[128,768]{1,0:T(8,128)(2,1)}) custom-call(bf16[256,2048]{1,0:T(8,128)(2,1)} %get-tuple-element.13.in_grad, bf16[8,256]{1,0:T(8,128)(2,1)} %get-tuple-element.14.gate_grad, ...), custom_call_target="tpu_custom_call" | custom-call | tf_op jit(solution)/shard_map/hand_over/pallas_call | solution.py:428
